TPU v7x, 32 devices: a whole 2x2x4 slice. The times are simulated.
32 devices in a mesh: orb: 4 (over z), box: 8 (over y, x, core).
Axes of the slice: x: 2, y: 2, z: 4, core: 2. Of those that a mesh axis runs over, the one named last changes fastest.
Arguments:
- coarse: bfloat16 [4, 8, 729, 1024], P('orb', None, None, 'box'), may hold values from -1.5 to 1.5
- wavelets: bfloat16 [4, 7, 729, 1024], P('orb', None, None, 'box'), may hold values from -1.5 to 1.5
- leaf_flags: int32 [4, 1024], P('orb', 'box'), may hold values 0 or 1
- child_key1: int32 [1024], P('box'), may hold values from 0 to 8191, as said below
- child_key2: int32 [2048], P('box'), may hold values from 0 to 8191, as said below
- counts: int32 [8], P('box'), may hold values from 128 to 256, as said below
Outputs:
- density: float32 [729, 2048], P(None, 'box')
Inputs may be any that keep to these rules, and one draw needn't show every extreme that they name: `child_key1`: within each curve range of 128 entries the keys rise and name distinct children; each parent lies in the same range or among the last 32 boxes of the range before; every range but the first has an entry naming a child of the first of those 32 boxes. `child_key2`: within each curve range of 256 entries the keys rise and name distinct children; each parent lies in the same range or among the last 32 boxes of the range before; every range but the first has an entry naming a child of the first of those 32 boxes. `counts`: some range is full in every draw and some range holds the fewest.
All inputs are finite; a program needn't handle non-finite values. No bound on the sum of `leaf_flags` on one device may be relied on, other than what follows from the above.
Results may differ from a plain program's by a relative error of at most 0.0003.
Values may be sent and summed in bfloat16 or wider, within the bound.
A program may use at most 64 MiB of HBM per device.

v0:
```python
import math

import jax
import jax.numpy as jnp
import numpy as np
from jax import lax
from jax.experimental import pallas as pl
from jax.experimental.pallas import tpu as pltpu
from jax.sharding import PartitionSpec as P

SPILL = 32


def legendre_pair(order, where):
    before = where * 0.0 + 1.0
    value = where
    for degree in range(1, order):
        before, value = (value, ((2 * degree + 1) * where * value - degree * before) / (degree + 1))
    return (value, before)


def gauss_rule(order):
    nodes = np.cos(np.pi * (np.arange(order) + 0.75) / (order + 0.5))
    for repeat in range(40):
        value, before = legendre_pair(order, nodes)
        slope = order * (nodes * value - before) / (nodes * nodes - 1.0)
        nodes = nodes - value / slope
    value, before = legendre_pair(order, nodes)
    slope = order * (nodes * value - before) / (nodes * nodes - 1.0)
    weights = 2.0 / ((1.0 - nodes * nodes) * slope * slope)
    return (nodes[::-1], weights[::-1])


def legendre_basis(where):
    shifted = 2.0 * where - 1.0
    rows = [shifted * 0.0 + 1.0, shifted]
    for degree in range(1, 8):
        rows.append(
            ((2 * degree + 1) * shifted * rows[degree] - degree * rows[degree - 1]) / (degree + 1)
        )
    scale = np.sqrt(2.0 * np.arange(9) + 1.0)[:, None]
    return np.stack(rows, 0) * scale


def complement_rows(scaling_rows):
    members = [scaling_rows[index] for index in range(9)]
    kept = []
    identity = np.eye(18)
    for column in range(18):
        vector = identity[column]
        for passes in range(2):
            for member in members + kept:
                vector = vector - np.dot(member, vector) * member
        length = np.sqrt(np.dot(vector, vector))
        if length > 0.1 and len(kept) < 9:
            kept.append(vector / length)
    return np.stack(kept, 0)


def wavelet_tables():
    nodes, weights = gauss_rule(24)
    points = 0.5 * (nodes + 1.0)
    halves = 0.5 * weights
    lower = legendre_basis(0.5 * points) * halves @ legendre_basis(points).T / math.sqrt(2.0)
    upper = legendre_basis(0.5 * points + 0.5) * halves @ legendre_basis(points).T / math.sqrt(2.0)
    scaling_rows = np.concatenate([lower, upper], 1)
    wavelet_rows = complement_rows(scaling_rows)
    matrix = np.concatenate([scaling_rows, wavelet_rows], 0).reshape(2, 9, 2, 9)
    gauss, gauss_weights = gauss_rule(9)
    quad = legendre_basis(0.5 * (gauss + 1.0)).T * np.sqrt(0.5 * gauss_weights)[:, None]
    return (matrix.reshape(18, 2, 9), quad)


ROWS = 729
PADDED = 800
SEGMENT = 92
HALVES = (((0, 1), (2, 3, 4)), ((5, 6), (7, 8), (9, 10)))
GROUPS = ((0, 1), (2, 3), (4, 5), (6, 7), (8, 9, 10))
QUARTER = 192


def local_keys(keys, boxes):
    key = keys - lax.axis_index("box") * (8 * boxes)
    return (lax.shift_right_arithmetic(key, 3), key & 7)


def spread_matrix(boxes, group):
    source = lax.broadcasted_iota(jnp.int32, (boxes, 128), 0)
    target = lax.broadcasted_iota(jnp.int32, (boxes, 128), 1)
    hit = (source - (boxes - SPILL) == target - SPILL * group) & (source >= boxes - SPILL)
    return hit.astype(jnp.float32).astype(jnp.bfloat16)


def pick_own(column, boxes):
    row = lax.broadcasted_iota(jnp.int32, (boxes, column.shape[1]), 0)
    return (row == column).astype(jnp.float32)


def pick_spilled(column, group):
    row = lax.broadcasted_iota(jnp.int32, (128, column.shape[1]), 0)
    hit = (row == column + SPILL * (group + 1)) & (column < 0)
    return hit.astype(jnp.float32)


def fill_coefficients(coef_ref, octant, table):
    for axis in range(3):
        bit = jnp.broadcast_to((octant >> axis) & 1, (8, 128)) == 1
        for k in range(18):
            for f in range(9):
                coef_ref[axis * 162 + k * 9 + f] = jnp.where(
                    bit, np.float32(table[k, 1, f]), np.float32(table[k, 0, f])
                )


def contract(source_ref, low, high, coef_ref, axis, store, groups=GROUPS):
    def load(block, row):
        if len(source_ref.shape) == 2:
            return source_ref[pl.ds(8 * row + block, 8, stride=72), :]
        return source_ref[block, pl.ds(row, 8, stride=9), :]

    for group in groups:
        inputs = [[load(block, l + 72 * t) for block in (low, high) for l in range(9)] for t in group]
        for f in range(9):
            sums = [None] * len(group)
            for k in range(18):
                weight = coef_ref[axis * 162 + k * 9 + f]
                for n in range(len(group)):
                    term = weight * inputs[n][k]
                    sums[n] = term if sums[n] is None else sums[n] + term
            for n, t in enumerate(group):
                store(81 * f + 8 * t, min(8, 81 - 8 * t), sums[n])


def lower_axis(source_ref, target_ref, coef_ref, axis, start, stop, groups=GROUPS):
    def step(index, carry):
        def store(row, count, value):
            target_ref[index, row : row + count, :] = value[:count]

        contract(source_ref, 2 * index, 2 * index + 1, coef_ref, axis, store, groups)
        return carry

    lax.fori_loop(start, stop, step, 0)


def dot(left, right):
    return jnp.dot(left, right, preferred_element_type=jnp.float32)


def encode(value):
    top = jnp.max(jnp.abs(value), axis=0, keepdims=True)
    scaled = value * (32767.0 / jnp.maximum(top, 1e-30))
    return (jnp.round(scaled).astype(jnp.int32).astype(jnp.int16), top)


def decode_square(code, top):
    value = code.astype(jnp.int32).astype(jnp.float32) * (top * np.float32(1.0 / 32767.0))
    return value * value


def density_kernel(
    counts_ref, coarse_hbm, waves_hbm, flags_ref, key1_ref, key2_ref, sum_code, sum_top,
    coarse_ref, waves_ref, coarse_pack_ref, coarse_halo_ref, pack_ref, halo_ref, level_ref, fine_ref, spill_ref, spilled_ref,
    x_ref, a_ref, b_ref, coef_ref, value_ref, code_ref, top_ref,
    got_code, got_top, load_sem, halo_send, halo_recv, code_send, code_recv, top_send, top_recv,
    sum_send, sum_recv, peak_send, peak_recv, *, count, ranges, table, valued
):
    boxes = coarse_hbm.shape[-1]
    tiles, padded = code_ref.shape[:2]
    chunk = padded // count
    me, position = lax.axis_index("orb"), lax.axis_index("box")
    after, before = lax.rem(position + 1, ranges), lax.rem(position + ranges - 1, ranges)
    mesh_id = pl.DeviceIdType.MESH
    load_coarse = pltpu.make_async_copy(coarse_hbm, coarse_ref.at[pl.ds(0, ROWS)], load_sem.at[0])
    load_waves = pltpu.make_async_copy(waves_hbm, waves_ref, load_sem.at[1])
    load_coarse.start()
    load_waves.start()
    barrier = pltpu.get_barrier_semaphore()
    for d in range(1, count):
        pl.semaphore_signal(barrier, inc=1, device_id={"orb": lax.rem(me + d, count)}, device_id_type=mesh_id)
    for other in (after, before):
        pl.semaphore_signal(barrier, inc=1, device_id={"box": other}, device_id_type=mesh_id)

    def halo(source, target, index):
        return pltpu.make_async_remote_copy(
            src_ref=source,
            dst_ref=target,
            send_sem=halo_send.at[index],
            recv_sem=halo_recv.at[index],
            device_id={"box": after},
            device_id_type=mesh_id,
        )

    def direct(source, target, sends, recvs, d, t):
        return pltpu.make_async_remote_copy(
            src_ref=source,
            dst_ref=target,
            send_sem=sends.at[d - 1, t],
            recv_sem=recvs.at[d - 1, t],
            device_id={"orb": lax.rem(me + d, count)},
            device_id_type=mesh_id,
        )

    def rows(owner):
        return pl.ds(pl.multiple_of(owner * chunk, chunk), chunk)

    def partials(d, t):
        peer = lax.rem(me + d, count)
        return (
            direct(top_ref.at[t], got_top.at[d - 1, t], top_send, top_recv, d, t),
            direct(code_ref.at[t, rows(peer)], got_code.at[d - 1, t], code_send, code_recv, d, t),
        )

    def totals(d, t):
        return (
            direct(sum_top.at[me, t], sum_top.at[me, t], peak_send, peak_recv, d, t),
            direct(sum_code.at[me, t], sum_code.at[me, t], sum_send, sum_recv, d, t),
        )

    coarse_halo = [halo(coarse_pack_ref.at[h], coarse_halo_ref.at[h], h) for h in range(2)]
    waves_halo = halo(pack_ref, halo_ref, 2)
    fine_halo = halo(spill_ref, spilled_ref, 3)
    keep = jnp.broadcast_to((1 - flags_ref[...]).astype(jnp.float32), (16, boxes)).astype(jnp.bfloat16)
    spread = [spread_matrix(boxes, g) for g in range(4)]
    tail = 8 * SEGMENT - ROWS
    coarse_ref[ROWS : ROWS + tail] = jnp.zeros((tail, 8, boxes), jnp.bfloat16)

    def segment(index):
        return coarse_ref[SEGMENT * index : SEGMENT * (index + 1)].reshape(8 * SEGMENT, boxes)

    load_coarse.wait()
    for h in range(2):
        total = dot(segment(4 * h), spread[0])
        for g in range(1, 4):
            total = total + dot(segment(4 * h + g), spread[g])
        coarse_pack_ref[h] = total.astype(jnp.bfloat16)
        if h == 0:
            pl.semaphore_wait(barrier, count + 1)
        coarse_halo[h].start()
    load_waves.wait()
    packed_keep = sum(dot(keep, s) for s in spread)[:1]
    for h in range(2):
        total = None
        for g in range(4):
            if 4 * h + g > 0:
                term = dot(waves_ref[0, 4 * h + g - 1], spread[g])
                total = term if total is None else total + term
        pack_ref[h] = (total * packed_keep).astype(jnp.bfloat16)
    waves_halo.start()
    column, octant = local_keys(key1_ref[...], boxes)
    fill_coefficients(coef_ref.at[tiles], octant, table)
    own = pick_own(column, boxes)
    fine_ref[ROWS - 1 : 4 * QUARTER, :] = jnp.zeros((4 * QUARTER - ROWS + 1, 128), jnp.float32)
    value_ref[ROWS - 1 : padded, :] = jnp.zeros((padded - ROWS + 1, 128), jnp.float32)

    def leaf_coefficients(t, carry):
        fill_coefficients(coef_ref.at[t], local_keys(key2_ref[t], boxes)[1], valued)
        return carry

    lax.fori_loop(0, tiles, leaf_coefficients, 0)
    coef = coef_ref.at[tiles]
    for h in range(2):
        coarse_halo[h].wait_recv()
        for g in range(4):
            pick = jnp.concatenate([own, pick_spilled(column, g)], 0).astype(jnp.bfloat16)
            both = jnp.concatenate([segment(4 * h + g), coarse_halo_ref[h]], 1)
            start = 8 * SEGMENT * (4 * h + g)
            level_ref[start : start + 8 * SEGMENT, :] = dot(both, pick)
        lower_axis(level_ref, a_ref, coef, 0, 0, 4, HALVES[h])
    lower_axis(a_ref, b_ref, coef, 1, 0, 2)

    def store_fine(row, rows_in, value):
        fine_ref[row : row + rows_in, :] = value[:rows_in]

    contract(b_ref, 0, 1, coef, 2, store_fine)
    for part in range(2):
        total = None
        for g in range(4):
            quarter = fine_ref[QUARTER * g : QUARTER * (g + 1), :]
            half = quarter.astype(jnp.bfloat16)
            if part == 1:
                half = (quarter - half.astype(jnp.float32)).astype(jnp.bfloat16)
            term = dot(half, spread[g])
            total = term if total is None else total + term
        spill_ref[part] = total.astype(jnp.bfloat16)
    fine_halo.start()

    def leaf_tile(t, carry):
        column = local_keys(key2_ref[t], boxes)[0]
        coef = coef_ref.at[t]
        own = pick_own(column, boxes)
        own_kept = own * dot(keep, own.astype(jnp.bfloat16))[:1]

        @pl.when(t == 0)
        def arrived_waves():
            waves_halo.wait_recv()

        for g in range(4):
            pick = jnp.concatenate([own_kept, pick_spilled(column, g)], 0).astype(jnp.bfloat16)
            for h in range(2):
                if 4 * h + g > 0:
                    both = jnp.concatenate([waves_ref[0, 4 * h + g - 1], halo_ref[h]], 1)
                    x_ref[4 * h + g, 0:ROWS, :] = dot(both, pick)
        lower_axis(x_ref, a_ref, coef, 0, 1, 4)

        @pl.when(t == 0)
        def arrived_fine():
            fine_halo.wait_recv()

        for g in range(4):
            pick = jnp.concatenate([own, pick_spilled(column, g)], 0).astype(jnp.bfloat16)
            quarter = fine_ref[QUARTER * g : QUARTER * (g + 1), :]
            high = quarter.astype(jnp.bfloat16)
            low = (quarter - high.astype(jnp.float32)).astype(jnp.bfloat16)
            total = dot(jnp.concatenate([high, spilled_ref[0]], 1), pick)
            total = total + dot(jnp.concatenate([low, spilled_ref[1]], 1), pick)
            x_ref[0, QUARTER * g : QUARTER * (g + 1), :] = total
        lower_axis(x_ref, a_ref, coef, 0, 0, 1)
        lower_axis(a_ref, b_ref, coef, 1, 0, 2)
        slot = t * 128 + lax.broadcasted_iota(jnp.int32, (8, 128), 1)
        live = jnp.where(slot < counts_ref[0], 1.0, 0.0).astype(jnp.float32)

        def store_value(row, rows_in, value):
            value_ref[row : row + rows_in, :] = (value * live)[:rows_in]

        contract(b_ref, 0, 1, coef, 2, store_value)
        code, top = encode(value_ref[...])
        code_ref[t] = code
        top_ref[t] = jnp.broadcast_to(top, (8, 128))
        for d in range(1, count):
            for copy in partials(d, t):
                copy.start()
        return carry

    lax.fori_loop(0, tiles, leaf_tile, 0)
    for t in range(tiles):
        total = decode_square(code_ref[t, rows(me), :], top_ref[t, 0:1, :])
        for d in range(1, count):
            for copy in partials(d, t):
                copy.wait_recv()
            total = total + decode_square(got_code[d - 1, t], got_top[d - 1, t, 0:1, :])
        code, top = encode(jnp.sqrt(2.0 * total))
        sum_code[me, t] = code
        sum_top[me, t] = jnp.broadcast_to(top, (8, 128))
        for d in range(1, count):
            for copy in totals(d, t):
                copy.start()
    for t in range(tiles):
        for d in range(1, count):
            for copy in totals(d, t):
                copy.wait_recv()
    for copy in (*coarse_halo, waves_halo, fine_halo):
        copy.wait_send()
    for t in range(tiles):
        for d in range(1, count):
            for copy in partials(d, t) + totals(d, t):
                copy.wait_send()


def decode_kernel(code_ref, top_ref, out_ref):
    count, tiles, chunk = code_ref.shape[:3]
    for owner in range(count):
        rows = min(chunk, ROWS - owner * chunk)
        if rows > 0:
            for t in range(tiles):
                value = decode_square(code_ref[owner, t], top_ref[owner, t, 0:1, :])
                out_ref[owner * chunk : owner * chunk + rows, 128 * t : 128 * (t + 1)] = value[:rows]


def shards(coarse, wavelets, leaf_flags, child_key1, child_key2, counts):
    matrix, quad = wavelet_tables()
    valued = np.einsum("kop,gp->kog", matrix, quad)
    boxes = coarse.shape[-1]
    slots = child_key2.shape[0]
    count, ranges = lax.axis_size("orb"), lax.axis_size("box")
    padded = -(-ROWS // (16 * count)) * 16 * count
    chunk = padded // count
    tiles = slots // 128
    peers = (count - 1, tiles)
    vmem = pl.BlockSpec(memory_space=pltpu.VMEM)
    anywhere = pl.BlockSpec(memory_space=pltpu.HBM)
    codes, tops = pl.pallas_call(
        lambda *refs: density_kernel(*refs, count=count, ranges=ranges, table=matrix, valued=valued),
        out_shape=(
            jax.ShapeDtypeStruct((count, tiles, chunk, 128), jnp.int16),
            jax.ShapeDtypeStruct((count, tiles, 8, 128), jnp.float32),
        ),
        in_specs=[pl.BlockSpec(memory_space=pltpu.SMEM), anywhere, anywhere, vmem, vmem, vmem],
        out_specs=(vmem, vmem),
        scratch_shapes=[
            pltpu.VMEM((8 * SEGMENT, 8, boxes), jnp.bfloat16),
            pltpu.VMEM(wavelets.shape, jnp.bfloat16),
            pltpu.VMEM((2, 8 * SEGMENT, 128), jnp.bfloat16),
            pltpu.VMEM((2, 8 * SEGMENT, 128), jnp.bfloat16),
            pltpu.VMEM((2, ROWS, 128), jnp.bfloat16),
            pltpu.VMEM((2, ROWS, 128), jnp.bfloat16),
            pltpu.VMEM((8 * PADDED, 128), jnp.float32),
            pltpu.VMEM((4 * QUARTER, 128), jnp.float32),
            pltpu.VMEM((2, QUARTER, 128), jnp.bfloat16),
            pltpu.VMEM((2, QUARTER, 128), jnp.bfloat16),
            pltpu.VMEM((8, PADDED, 128), jnp.float32),
            pltpu.VMEM((4, PADDED, 128), jnp.float32),
            pltpu.VMEM((2, PADDED, 128), jnp.float32),
            pltpu.VMEM((tiles + 1, 3 * 162, 8, 128), jnp.float32),
            pltpu.VMEM((padded, 128), jnp.float32),
            pltpu.VMEM((tiles, padded, 128), jnp.int16),
            pltpu.VMEM((tiles, 8, 128), jnp.float32),
            pltpu.VMEM(peers + (chunk, 128), jnp.int16),
            pltpu.VMEM(peers + (8, 128), jnp.float32),
            pltpu.SemaphoreType.DMA((2,)),
            pltpu.SemaphoreType.DMA((4,)),
            pltpu.SemaphoreType.DMA((4,)),
        ]
        + [pltpu.SemaphoreType.DMA(peers)] * 8,
        compiler_params=pltpu.CompilerParams(
            collective_id=0, has_side_effects=True, vmem_limit_bytes=60 * 1024 * 1024
        ),
    )(
        counts,
        jnp.transpose(coarse[0], (1, 0, 2)),
        wavelets,
        leaf_flags,
        child_key1.reshape(1, boxes),
        child_key2.reshape(tiles, 1, 128),
    )
    return pl.pallas_call(
        decode_kernel,
        out_shape=jax.ShapeDtypeStruct((ROWS, slots), jnp.float32),
        in_specs=[vmem] * 2,
        out_specs=vmem,
    )(codes, tops)


def solution(mesh):
    in_specs = (
        P("orb", None, None, "box"),
        P("orb", None, None, "box"),
        P("orb", "box"),
        P("box"),
        P("box"),
        P("box"),
    )
    out_specs = P(None, "box")
    return jax.shard_map(shards, mesh=mesh, in_specs=in_specs, out_specs=out_specs, check_vma=False)
```

profile of v0, /device:TPU:0, one launch (start us, length us, event | category | flops | bytes accessed | tf_op | source)
XLA Modules:
  0.0 44.6 jit_solution(6409632335728218379)
XLA Ops:
  0.7 42.0 %shard_map.64 = (s16[4,2,192,128]{3,2,1,0:T(8,128)(2,1)}, f32[4,2,8,128]{3,2,1,0:T(8,128)}) custom-call(s32[1]{0:T(128)S(6)} %copy.7.refs_0_, bf16[729,8,128]{2,1,0:T(8,128)(2,1)} %bitcast.5, bf16[1,7,729,128]{3,2,1,0:T(8,128)(2,1)} %refs_2_.1, s32[1,128]{1,0:T(1,128)} %refs_3_.1, s32[1,128]{1,0:T(1,128)} %bitcast.7, s32[2,1,128]{2,1,0:T(1,128)} %bitcast.6), custom_call_target="tpu_custom_call" | custom-call | tf_op jit(solution)/shard_map/pallas_call | solution.py:381
  42.6 2.0 %shard_map.65 = f32[729,256]{1,0:T(8,128)} custom-call(s16[4,2,192,128]{3,2,1,0:T(8,128)(2,1)} %get-tuple-element.7.code_ref, f32[4,2,8,128]{3,2,1,0:T(8,128)} %get-tuple-element.8.top_ref), custom_call_target="tpu_custom_call" | custom-call | tf_op jit(solution)/shard_map/pallas_call | solution.py:425
where the time goes:
time: 44.8 us; the launch traced here: 44.6 us
  Pallas kernels  44 us (98%)
  between operations  0.66 us (1%)
    pallas_call x1, Pallas kernels, shards(): pl.pallas_call(lambda *refs: density_kernel(*refs, count=count, ranges=ra...  42 us
    pallas_call x1, Pallas kernels, shards(): pl.pallas_call(decode_kernel, out_shape=jax.ShapeDtypeStruct((ROWS, slots...  1.97 us

commit v1 on v0

v1 whole, which is shorter than its diff:
```python
import math

import jax
import jax.numpy as jnp
import numpy as np
from jax import lax
from jax.experimental import pallas as pl
from jax.experimental.pallas import tpu as pltpu
from jax.sharding import PartitionSpec as P

SPILL = 32


def legendre_pair(order, where):
    before = where * 0.0 + 1.0
    value = where
    for degree in range(1, order):
        before, value = (value, ((2 * degree + 1) * where * value - degree * before) / (degree + 1))
    return (value, before)


def gauss_rule(order):
    nodes = np.cos(np.pi * (np.arange(order) + 0.75) / (order + 0.5))
    for repeat in range(40):
        value, before = legendre_pair(order, nodes)
        slope = order * (nodes * value - before) / (nodes * nodes - 1.0)
        nodes = nodes - value / slope
    value, before = legendre_pair(order, nodes)
    slope = order * (nodes * value - before) / (nodes * nodes - 1.0)
    weights = 2.0 / ((1.0 - nodes * nodes) * slope * slope)
    return (nodes[::-1], weights[::-1])


def legendre_basis(where):
    shifted = 2.0 * where - 1.0
    rows = [shifted * 0.0 + 1.0, shifted]
    for degree in range(1, 8):
        rows.append(
            ((2 * degree + 1) * shifted * rows[degree] - degree * rows[degree - 1]) / (degree + 1)
        )
    scale = np.sqrt(2.0 * np.arange(9) + 1.0)[:, None]
    return np.stack(rows, 0) * scale


def complement_rows(scaling_rows):
    members = [scaling_rows[index] for index in range(9)]
    kept = []
    identity = np.eye(18)
    for column in range(18):
        vector = identity[column]
        for passes in range(2):
            for member in members + kept:
                vector = vector - np.dot(member, vector) * member
        length = np.sqrt(np.dot(vector, vector))
        if length > 0.1 and len(kept) < 9:
            kept.append(vector / length)
    return np.stack(kept, 0)


def wavelet_tables():
    nodes, weights = gauss_rule(24)
    points = 0.5 * (nodes + 1.0)
    halves = 0.5 * weights
    lower = legendre_basis(0.5 * points) * halves @ legendre_basis(points).T / math.sqrt(2.0)
    upper = legendre_basis(0.5 * points + 0.5) * halves @ legendre_basis(points).T / math.sqrt(2.0)
    scaling_rows = np.concatenate([lower, upper], 1)
    wavelet_rows = complement_rows(scaling_rows)
    matrix = np.concatenate([scaling_rows, wavelet_rows], 0).reshape(2, 9, 2, 9)
    gauss, gauss_weights = gauss_rule(9)
    quad = legendre_basis(0.5 * (gauss + 1.0)).T * np.sqrt(0.5 * gauss_weights)[:, None]
    return (matrix.reshape(18, 2, 9), quad)


ROWS = 729
PADDED = 800
SEGMENT = 92
HALVES = (((0, 1), (2, 3, 4)), ((5, 6), (7, 8), (9, 10)))
GROUPS = ((0, 1), (2, 3), (4, 5), (6, 7), (8, 9, 10))
THIRD_GROUPS = ((0, 1), (2, 3))
QUARTER = 192
PARTS = 3
WIDTH = 27
PIECE = 243
PIECE_ROWS = 256
SCALE_ROW = 248
PART_ROWS = 288
LAG = 2


def local_keys(keys, boxes):
    key = keys - lax.axis_index("box") * (8 * boxes)
    return (lax.shift_right_arithmetic(key, 3), key & 7)


def spread_matrix(boxes, group):
    source = lax.broadcasted_iota(jnp.int32, (boxes, 128), 0)
    target = lax.broadcasted_iota(jnp.int32, (boxes, 128), 1)
    hit = (source - (boxes - SPILL) == target - SPILL * group) & (source >= boxes - SPILL)
    return hit.astype(jnp.float32).astype(jnp.bfloat16)


def pick_own(column, boxes):
    row = lax.broadcasted_iota(jnp.int32, (boxes, column.shape[1]), 0)
    return (row == column).astype(jnp.float32)


def pick_spilled(column, group):
    row = lax.broadcasted_iota(jnp.int32, (128, column.shape[1]), 0)
    hit = (row == column + SPILL * (group + 1)) & (column < 0)
    return hit.astype(jnp.float32)


def fill_coefficients(coef_ref, octant, table):
    for axis in range(3):
        bit = jnp.broadcast_to((octant >> axis) & 1, (8, 128)) == 1
        for k in range(18):
            for f in range(9):
                coef_ref[axis * 162 + k * 9 + f] = jnp.where(
                    bit, np.float32(table[k, 1, f]), np.float32(table[k, 0, f])
                )


def contract(source_ref, low, high, coef_ref, axis, store, groups=GROUPS, first=0, outputs=9, width=81):
    def load(block, row):
        if len(source_ref.shape) == 2:
            return source_ref[pl.ds(8 * row + block, 8, stride=72), :]
        return source_ref[block, pl.ds(row, 8, stride=9), :]

    for group in groups:
        inputs = [[load(block, l + 72 * t) for block in (low, high) for l in range(9)] for t in group]
        for f in range(outputs):
            sums = [None] * len(group)
            for k in range(18):
                weight = coef_ref[axis * 162 + k * 9 + first + f]
                for n in range(len(group)):
                    term = weight * inputs[n][k]
                    sums[n] = term if sums[n] is None else sums[n] + term
            for n, t in enumerate(group):
                store(width * f + 8 * t, min(8, width - 8 * t), sums[n])


def lower_axis(source_ref, target_ref, coef_ref, axis, start, stop, groups=GROUPS, **kinds):
    def step(index, carry):
        def store(row, count, value):
            target_ref[index, row : row + count, :] = value[:count]

        contract(source_ref, 2 * index, 2 * index + 1, coef_ref, axis, store, groups, **kinds)
        return carry

    lax.fori_loop(start, stop, step, 0)


def dot(left, right):
    return jnp.dot(left, right, preferred_element_type=jnp.float32)


def scale_of(steps):
    return jnp.exp2(steps * np.float32(1.0 / 256.0))


def encode(value):
    top = jnp.maximum(jnp.max(jnp.abs(value), axis=0, keepdims=True), 1e-30)
    steps = jnp.ceil(jnp.log2(top) * 256.0)
    code = jnp.round(value[:SCALE_ROW] * (32700.0 / scale_of(steps)))
    code = jnp.concatenate([code, jnp.broadcast_to(steps, (PIECE_ROWS - SCALE_ROW, 128))], 0)
    return code.astype(jnp.int32).astype(jnp.int16)


def decode_square(code):
    code = code.astype(jnp.int32).astype(jnp.float32)
    value = code[:SCALE_ROW] * (scale_of(code[SCALE_ROW : SCALE_ROW + 1]) * np.float32(1.0 / 32700.0))
    return value * value


def full_rows(value):
    return jnp.concatenate([value, jnp.zeros((PIECE_ROWS - SCALE_ROW, 128), jnp.float32)], 0)


def density_kernel(
    counts_ref, coarse_hbm, waves_hbm, flags_ref, key1_ref, key2_ref, sum_code,
    coarse_ref, waves_ref, coarse_pack_ref, coarse_halo_ref, pack_ref, halo_ref, level_ref, fine_ref, spill_ref, spilled_ref,
    x_ref, a_ref, b_ref, part_a_ref, part_b_ref, coef_ref, value_ref, code_ref, got_outer, got_middle,
    load_sem, halo_send, halo_recv, code_send, outer_recv, middle_recv, sum_send, sum_recv, *, count, ranges, table, valued
):
    boxes = coarse_hbm.shape[-1]
    pieces = code_ref.shape[0]
    tiles = pieces // PARTS
    me, position = lax.axis_index("orb"), lax.axis_index("box")
    after, before = lax.rem(position + 1, ranges), lax.rem(position + ranges - 1, ranges)
    half = count // 2
    inward = jnp.where(me < half, me + 1, me - 1)
    outward = jnp.where(me < half, me - 1, me + 1)
    outermost = (me == 0) | (me == count - 1)
    middle = (me == half - 1) | (me == half)
    first_range, last_range = position == 0, position == ranges - 1
    mesh_id = pl.DeviceIdType.MESH
    load_coarse = pltpu.make_async_copy(coarse_hbm, coarse_ref.at[pl.ds(0, ROWS)], load_sem.at[0])
    load_waves = pltpu.make_async_copy(waves_hbm, waves_ref, load_sem.at[1])
    load_coarse.start()
    load_waves.start()
    barrier = pltpu.get_barrier_semaphore()
    for d in range(1, count):
        pl.semaphore_signal(barrier, inc=1, device_id={"orb": lax.rem(me + d, count)}, device_id_type=mesh_id)
    for other in (after, before):
        pl.semaphore_signal(barrier, inc=1, device_id={"box": other}, device_id_type=mesh_id)

    def remote(source, target, sends, recvs, device):
        return pltpu.make_async_remote_copy(
            src_ref=source,
            dst_ref=target,
            send_sem=sends,
            recv_sem=recvs,
            device_id=device,
            device_id_type=mesh_id,
        )

    def halo(source, target, index):
        return remote(source, target, halo_send.at[index], halo_recv.at[index], {"box": after})

    def to_outer_slot(n):
        return remote(code_ref.at[n], got_outer.at[n], code_send.at[n], outer_recv.at[n], {"orb": inward})

    def to_middle_slot(n):
        return remote(code_ref.at[n], got_middle.at[n], code_send.at[n], middle_recv.at[n], {"orb": inward})

    def to_total(n):
        return remote(sum_code.at[n], sum_code.at[n], sum_send.at[n], sum_recv.at[n], {"orb": outward})

    def when_not(condition):
        return pl.when(jnp.logical_not(condition))

    def send_halo(copy):
        @when_not(last_range)
        def send():
            copy.start()

    def wait_halo(copy):
        @when_not(first_range)
        def wait():
            copy.wait_recv()

    def send_partial(n, value):
        code_ref[n] = encode(value)

        @pl.when(middle)
        def exchange():
            to_middle_slot(n).start()

        @when_not(middle)
        def pass_in():
            to_outer_slot(n).start()

    def combine(n):
        @when_not(outermost)
        def add():
            to_outer_slot(n).wait_recv()
            own = value_ref[n]
            total = full_rows(decode_square(got_outer[n])) + own * own
            send_partial(n, jnp.sqrt(total))

    def finish(n):
        @pl.when(middle)
        def close():
            to_middle_slot(n).wait_recv()
            total = decode_square(code_ref[n]) + decode_square(got_middle[n])
            sum_code[n] = encode(full_rows(jnp.sqrt(2.0 * total)))

        @when_not(middle | outermost)
        def receive():
            to_total(n).wait_recv()

        @when_not(outermost)
        def pass_out():
            to_total(n).start()

    coarse_halo = [halo(coarse_pack_ref.at[h], coarse_halo_ref.at[h], h) for h in range(2)]
    waves_halo = halo(pack_ref, halo_ref, 2)
    fine_halo = halo(spill_ref, spilled_ref, 3)

    @pl.when(first_range)
    def no_halo():
        for ref in (coarse_halo_ref, halo_ref, spilled_ref):
            ref[...] = jnp.zeros(ref.shape, ref.dtype)

    keep = jnp.broadcast_to((1 - flags_ref[...]).astype(jnp.float32), (16, boxes)).astype(jnp.bfloat16)
    spread = [spread_matrix(boxes, g) for g in range(4)]
    tail = 8 * SEGMENT - ROWS
    coarse_ref[ROWS : ROWS + tail] = jnp.zeros((tail, 8, boxes), jnp.bfloat16)

    def segment(index):
        return coarse_ref[SEGMENT * index : SEGMENT * (index + 1)].reshape(8 * SEGMENT, boxes)

    load_coarse.wait()
    for h in range(2):
        total = dot(segment(4 * h), spread[0])
        for g in range(1, 4):
            total = total + dot(segment(4 * h + g), spread[g])
        coarse_pack_ref[h] = total.astype(jnp.bfloat16)
        if h == 0:
            pl.semaphore_wait(barrier, count + 1)
        send_halo(coarse_halo[h])
    load_waves.wait()
    packed_keep = sum(dot(keep, s) for s in spread)[:1]
    for h in range(2):
        total = None
        for g in range(4):
            if 4 * h + g > 0:
                term = dot(waves_ref[0, 4 * h + g - 1], spread[g])
                total = term if total is None else total + term
        pack_ref[h] = (total * packed_keep).astype(jnp.bfloat16)
    send_halo(waves_halo)
    column, octant = local_keys(key1_ref[...], boxes)
    fill_coefficients(coef_ref.at[tiles], octant, table)
    own = pick_own(column, boxes)
    fine_ref[ROWS - 1 : 4 * QUARTER, :] = jnp.zeros((4 * QUARTER - ROWS + 1, 128), jnp.float32)
    pad = PIECE_ROWS - PIECE + 3
    value_ref[:, PIECE_ROWS - pad : PIECE_ROWS, :] = jnp.zeros((pieces, pad, 128), jnp.float32)

    def leaf_coefficients(t, carry):
        fill_coefficients(coef_ref.at[t], local_keys(key2_ref[t], boxes)[1], valued)
        return carry

    lax.fori_loop(0, tiles, leaf_coefficients, 0)
    coef = coef_ref.at[tiles]
    for h in range(2):
        wait_halo(coarse_halo[h])
        for g in range(4):
            pick = jnp.concatenate([own, pick_spilled(column, g)], 0).astype(jnp.bfloat16)
            both = jnp.concatenate([segment(4 * h + g), coarse_halo_ref[h]], 1)
            start = 8 * SEGMENT * (4 * h + g)
            level_ref[start : start + 8 * SEGMENT, :] = dot(both, pick)
        lower_axis(level_ref, a_ref, coef, 0, 0, 4, HALVES[h])
    lower_axis(a_ref, b_ref, coef, 1, 0, 2)

    def store_fine(row, rows_in, value):
        fine_ref[row : row + rows_in, :] = value[:rows_in]

    contract(b_ref, 0, 1, coef, 2, store_fine)
    for part in range(2):
        total = None
        for g in range(4):
            quarter = fine_ref[QUARTER * g : QUARTER * (g + 1), :]
            half_value = quarter.astype(jnp.bfloat16)
            if part == 1:
                half_value = (quarter - half_value.astype(jnp.float32)).astype(jnp.bfloat16)
            term = dot(half_value, spread[g])
            total = term if total is None else total + term
        spill_ref[part] = total.astype(jnp.bfloat16)
    send_halo(fine_halo)

    columns = jnp.concatenate([local_keys(key2_ref[t], boxes)[0] for t in range(tiles)], 1)
    own = pick_own(columns, boxes)
    own_kept = own * dot(keep, own.astype(jnp.bfloat16))[:1]

    def store_blocks(block, start, rows_in, value):
        for t in range(tiles):
            x_ref[t, block, start : start + rows_in, :] = value[:, 128 * t : 128 * (t + 1)]

    wait_halo(waves_halo)
    for g in range(4):
        pick = jnp.concatenate([own_kept, pick_spilled(columns, g)], 0).astype(jnp.bfloat16)
        for h in range(2):
            if 4 * h + g > 0:
                both = jnp.concatenate([waves_ref[0, 4 * h + g - 1], halo_ref[h]], 1)
                store_blocks(4 * h + g, 0, ROWS, dot(both, pick))

    def leaf_axis(t, part, start, stop):
        lower_axis(
            x_ref.at[t], part_a_ref.at[part], coef_ref.at[t], 0, start, stop, first=3 * part, outputs=3
        )

    for part in range(PARTS):
        leaf_axis(0, part, 1, 4)
    wait_halo(fine_halo)
    for g in range(4):
        pick = jnp.concatenate([own, pick_spilled(columns, g)], 0).astype(jnp.bfloat16)
        quarter = fine_ref[QUARTER * g : QUARTER * (g + 1), :]
        high = quarter.astype(jnp.bfloat16)
        low = (quarter - high.astype(jnp.float32)).astype(jnp.bfloat16)
        total = dot(jnp.concatenate([high, spilled_ref[0]], 1), pick)
        total = total + dot(jnp.concatenate([low, spilled_ref[1]], 1), pick)
        store_blocks(0, QUARTER * g, QUARTER, total)
    for n in range(pieces):
        t, part = n // PARTS, n % PARTS
        leaf_axis(t, part, 0, 1 if t == 0 else 4)
        kinds = dict(groups=THIRD_GROUPS, width=WIDTH)
        lower_axis(part_a_ref.at[part], part_b_ref, coef_ref.at[t], 1, 0, 2, **kinds)
        slot = t * 128 + lax.broadcasted_iota(jnp.int32, (8, 128), 1)
        live = jnp.where(slot < counts_ref[0], 1.0, 0.0).astype(jnp.float32)

        def store_value(row, rows_in, value):
            value_ref[n, row : row + rows_in, :] = (value * live)[:rows_in]

        contract(part_b_ref, 0, 1, coef_ref.at[t], 2, store_value, **kinds)

        @pl.when(outermost)
        def start_chain():
            send_partial(n, value_ref[n])

        if n >= LAG:
            combine(n - LAG)
        if n >= 2 * LAG:
            finish(n - 2 * LAG)
    for n in range(pieces, pieces + 2 * LAG):
        if 0 <= n - LAG < pieces:
            combine(n - LAG)
        if 0 <= n - 2 * LAG:
            finish(n - 2 * LAG)

    @when_not(last_range)
    def halos_sent():
        for copy in (*coarse_halo, waves_halo, fine_halo):
            copy.wait_send()

    for n in range(pieces):
        to_outer_slot(n).wait_send()

        @when_not(outermost)
        def totals_sent():
            to_total(n).wait_send()

        @pl.when(outermost & jnp.logical_not(middle))
        def totals_received():
            to_total(n).wait_recv()


def decode_kernel(code_ref, out_hbm, piece_ref, value_ref, sem):
    pieces = code_ref.shape[0]
    tiles = pieces // PARTS

    def out_copy(t):
        return pltpu.make_async_copy(
            value_ref.at[t, pl.ds(0, ROWS)], out_hbm.at[:, pl.ds(128 * t, 128)], sem.at[t]
        )

    for n in range(pieces):
        piece_ref[n, 0:SCALE_ROW, :] = decode_square(code_ref[n])
    for n in range(pieces):
        t, part = n // PARTS, n % PARTS
        for f in range(3):
            for k in range(11):
                rows = min(8, 81 - 8 * k)
                value = piece_ref[n, pl.ds(24 * k + f, rows, stride=3), :]
                value_ref[t, pl.ds(72 * k + 3 * part + f, rows, stride=9), :] = value
        if part == PARTS - 1:
            out_copy(t).start()
    for t in range(tiles):
        out_copy(t).wait()


def shards(coarse, wavelets, leaf_flags, child_key1, child_key2, counts):
    matrix, quad = wavelet_tables()
    valued = np.einsum("kop,gp->kog", matrix, quad)
    boxes = coarse.shape[-1]
    slots = child_key2.shape[0]
    count, ranges = lax.axis_size("orb"), lax.axis_size("box")
    tiles = slots // 128
    pieces = PARTS * tiles
    vmem = pl.BlockSpec(memory_space=pltpu.VMEM)
    anywhere = pl.BlockSpec(memory_space=pltpu.HBM)
    codes = pl.pallas_call(
        lambda *refs: density_kernel(*refs, count=count, ranges=ranges, table=matrix, valued=valued),
        out_shape=jax.ShapeDtypeStruct((pieces, PIECE_ROWS, 128), jnp.int16),
        in_specs=[pl.BlockSpec(memory_space=pltpu.SMEM), anywhere, anywhere, vmem, vmem, vmem],
        out_specs=vmem,
        scratch_shapes=[
            pltpu.VMEM((8 * SEGMENT, 8, boxes), jnp.bfloat16),
            pltpu.VMEM(wavelets.shape, jnp.bfloat16),
            pltpu.VMEM((2, 8 * SEGMENT, 128), jnp.bfloat16),
            pltpu.VMEM((2, 8 * SEGMENT, 128), jnp.bfloat16),
            pltpu.VMEM((2, ROWS, 128), jnp.bfloat16),
            pltpu.VMEM((2, ROWS, 128), jnp.bfloat16),
            pltpu.VMEM((8 * PADDED, 128), jnp.float32),
            pltpu.VMEM((4 * QUARTER, 128), jnp.float32),
            pltpu.VMEM((2, QUARTER, 128), jnp.bfloat16),
            pltpu.VMEM((2, QUARTER, 128), jnp.bfloat16),
            pltpu.VMEM((tiles, 8, PADDED, 128), jnp.float32),
            pltpu.VMEM((4, PADDED, 128), jnp.float32),
            pltpu.VMEM((2, PADDED, 128), jnp.float32),
            pltpu.VMEM((PARTS, 4, PART_ROWS, 128), jnp.float32),
            pltpu.VMEM((2, PART_ROWS, 128), jnp.float32),
            pltpu.VMEM((tiles + 1, 3 * 162, 8, 128), jnp.float32),
            pltpu.VMEM((pieces, PIECE_ROWS, 128), jnp.float32),
            pltpu.VMEM((pieces, PIECE_ROWS, 128), jnp.int16),
            pltpu.VMEM((pieces, PIECE_ROWS, 128), jnp.int16),
            pltpu.VMEM((pieces, PIECE_ROWS, 128), jnp.int16),
            pltpu.SemaphoreType.DMA((2,)),
            pltpu.SemaphoreType.DMA((4,)),
            pltpu.SemaphoreType.DMA((4,)),
        ]
        + [pltpu.SemaphoreType.DMA((pieces,))] * 5,
        compiler_params=pltpu.CompilerParams(
            collective_id=0, has_side_effects=True, vmem_limit_bytes=60 * 1024 * 1024
        ),
    )(
        counts,
        jnp.transpose(coarse[0], (1, 0, 2)),
        wavelets,
        leaf_flags,
        child_key1.reshape(1, boxes),
        child_key2.reshape(tiles, 1, 128),
    )
    return pl.pallas_call(
        decode_kernel,
        out_shape=jax.ShapeDtypeStruct((ROWS, slots), jnp.float32),
        in_specs=[vmem],
        out_specs=anywhere,
        scratch_shapes=[
            pltpu.VMEM((pieces, PIECE_ROWS, 128), jnp.float32),
            pltpu.VMEM((tiles, PADDED, 128), jnp.float32),
            pltpu.SemaphoreType.DMA((tiles,)),
        ],
    )(codes)


def solution(mesh):
    in_specs = (
        P("orb", None, None, "box"),
        P("orb", None, None, "box"),
        P("orb", "box"),
        P("box"),
        P("box"),
        P("box"),
    )
    out_specs = P(None, "box")
    return jax.shard_map(shards, mesh=mesh, in_specs=in_specs, out_specs=out_specs, check_vma=False)
```

time: 44.8 us -> 39 us (0.87)
  the two profiles are of different devices: /device:TPU:0 before, /device:TPU:4 now
where the time goes in v1:
time: 39 us; the launch traced here: 38.8 us
  Pallas kernels  38.1 us (98%)
  between operations  0.66 us (2%)
    pallas_call x1, Pallas kernels, shards(): pl.pallas_call(lambda *refs: density_kernel(*refs, count=count, ranges=ra...  36.1 us
    pallas_call x1, Pallas kernels, shards(): pl.pallas_call(decode_kernel, out_shape=jax.ShapeDtypeStruct((ROWS, slots...  1.96 us

profile of v1, /device:TPU:4, one launch (start us, length us, event | category | flops | bytes accessed | tf_op | source)
XLA Modules:
  0.0 38.8 jit_solution(12253812402505805011)
XLA Ops:
  0.7 36.1 %shard_map.64.code_ref = s16[6,256,128]{2,1,0:T(8,128)(2,1)} custom-call(s32[1]{0:T(128)S(6)} %copy.7.refs_0_, bf16[729,8,128]{2,1,0:T(8,128)(2,1)} %bitcast.5, bf16[1,7,729,128]{3,2,1,0:T(8,128)(2,1)} %refs_2_.1, s32[1,128]{1,0:T(1,128)} %refs_3_.1, s32[1,128]{1,0:T(1,128)} %bitcast.7, s32[2,1,128]{2,1,0:T(1,128)} %bitcast.6), custom_call_target="tpu_custom_call" | custom-call | tf_op jit(solution)/shard_map/pallas_call | solution.py:461
  36.8 2.0 %shard_map.65 = f32[729,256]{1,0:T(8,128)} custom-call(s16[6,256,128]{2,1,0:T(8,128)(2,1)} %shard_map.64.code_ref), custom_call_target="tpu_custom_call" | custom-call | tf_op jit(solution)/shard_map/pallas_call | solution.py:503

commit v2 on v1

--- a/solution.py
+++ b/solution.py
@@ -82,7 +82,8 @@
 WIDTH = 27
 PIECE = 243
 PIECE_ROWS = 256
-SCALE_ROW = 248
+SPLITS = ((0, 112), (112, 256))
+SHIFT = 4
 PART_ROWS = 288
 LAG = 2
 
@@ -159,21 +160,26 @@
 
 
 def encode(value):
+    rows = value.shape[0]
+    last = lax.broadcasted_iota(jnp.int32, (8, 128), 0) == 7
     top = jnp.maximum(jnp.max(jnp.abs(value), axis=0, keepdims=True), 1e-30)
     steps = jnp.ceil(jnp.log2(top) * 256.0)
-    code = jnp.round(value[:SCALE_ROW] * (32700.0 / scale_of(steps)))
-    code = jnp.concatenate([code, jnp.broadcast_to(steps, (PIECE_ROWS - SCALE_ROW, 128))], 0)
+    code = jnp.round(value * (32700.0 / scale_of(steps)))
+    code = jnp.concatenate([code[: rows - 8], jnp.where(last, steps, code[rows - 8 :])], 0)
     return code.astype(jnp.int32).astype(jnp.int16)
 
 
 def decode_square(code):
+    rows = code.shape[0]
+    last = lax.broadcasted_iota(jnp.int32, (8, 128), 0) == 7
     code = code.astype(jnp.int32).astype(jnp.float32)
-    value = code[:SCALE_ROW] * (scale_of(code[SCALE_ROW : SCALE_ROW + 1]) * np.float32(1.0 / 32700.0))
+    value = code * (scale_of(code[rows - 1 : rows]) * np.float32(1.0 / 32700.0))
+    value = jnp.concatenate([value[: rows - 8], jnp.where(last, 0.0, value[rows - 8 :])], 0)
     return value * value
 
 
-def full_rows(value):
-    return jnp.concatenate([value, jnp.zeros((PIECE_ROWS - SCALE_ROW, 128), jnp.float32)], 0)
+def spread_row(row):
+    return row + (SHIFT if row >= 4 * WIDTH else 0)
 
 
 def density_kernel(
@@ -199,10 +205,15 @@
     load_coarse.start()
     load_waves.start()
     barrier = pltpu.get_barrier_semaphore()
-    for d in range(1, count):
-        pl.semaphore_signal(barrier, inc=1, device_id={"orb": lax.rem(me + d, count)}, device_id_type=mesh_id)
-    for other in (after, before):
-        pl.semaphore_signal(barrier, inc=1, device_id={"box": other}, device_id_type=mesh_id)
+    pl.semaphore_signal(barrier, inc=1, device_id={"orb": inward}, device_id_type=mesh_id)
+
+    @pl.when(jnp.logical_not(outermost))
+    def greet_outward():
+        pl.semaphore_signal(barrier, inc=1, device_id={"orb": outward}, device_id_type=mesh_id)
+
+    @pl.when(jnp.logical_not(first_range))
+    def greet_before():
+        pl.semaphore_signal(barrier, inc=1, device_id={"box": before}, device_id_type=mesh_id)
 
     def remote(source, target, sends, recvs, device):
         return pltpu.make_async_remote_copy(
@@ -217,14 +228,21 @@
     def halo(source, target, index):
         return remote(source, target, halo_send.at[index], halo_recv.at[index], {"box": after})
 
-    def to_outer_slot(n):
-        return remote(code_ref.at[n], got_outer.at[n], code_send.at[n], outer_recv.at[n], {"orb": inward})
-
-    def to_middle_slot(n):
-        return remote(code_ref.at[n], got_middle.at[n], code_send.at[n], middle_recv.at[n], {"orb": inward})
-
-    def to_total(n):
-        return remote(sum_code.at[n], sum_code.at[n], sum_send.at[n], sum_recv.at[n], {"orb": outward})
+    def part_of(ref, n, s):
+        return ref.at[n, pl.ds(SPLITS[s][0], SPLITS[s][1] - SPLITS[s][0])]
+
+    def inner_copy(slots, recvs, n, s):
+        return remote(part_of(code_ref, n, s), part_of(slots, n, s), code_send.at[n, s], recvs.at[n, s], {"orb": inward})
+
+    def to_outer_slot(n, s):
+        return inner_copy(got_outer, outer_recv, n, s)
+
+    def to_middle_slot(n, s):
+        return inner_copy(got_middle, middle_recv, n, s)
+
+    def to_total(n, s):
+        part = part_of(sum_code, n, s)
+        return remote(part, part, sum_send.at[n, s], sum_recv.at[n, s], {"orb": outward})
 
     def when_not(condition):
         return pl.when(jnp.logical_not(condition))
@@ -239,39 +257,42 @@
         def wait():
             copy.wait_recv()
 
-    def send_partial(n, value):
-        code_ref[n] = encode(value)
+    def send_partial(n, s, value):
+        start, stop = SPLITS[s]
+        code_ref[n, start:stop] = encode(value)
 
         @pl.when(middle)
         def exchange():
-            to_middle_slot(n).start()
+            to_middle_slot(n, s).start()
 
         @when_not(middle)
         def pass_in():
-            to_outer_slot(n).start()
+            to_outer_slot(n, s).start()
 
     def combine(n):
         @when_not(outermost)
         def add():
-            to_outer_slot(n).wait_recv()
-            own = value_ref[n]
-            total = full_rows(decode_square(got_outer[n])) + own * own
-            send_partial(n, jnp.sqrt(total))
+            for s, (start, stop) in enumerate(SPLITS):
+                to_outer_slot(n, s).wait_recv()
+                own = value_ref[n, start:stop]
+                send_partial(n, s, jnp.sqrt(decode_square(got_outer[n, start:stop]) + own * own))
 
     def finish(n):
-        @pl.when(middle)
-        def close():
-            to_middle_slot(n).wait_recv()
-            total = decode_square(code_ref[n]) + decode_square(got_middle[n])
-            sum_code[n] = encode(full_rows(jnp.sqrt(2.0 * total)))
-
-        @when_not(middle | outermost)
-        def receive():
-            to_total(n).wait_recv()
-
-        @when_not(outermost)
-        def pass_out():
-            to_total(n).start()
+        for s, (start, stop) in enumerate(SPLITS):
+
+            @pl.when(middle)
+            def close():
+                to_middle_slot(n, s).wait_recv()
+                total = decode_square(code_ref[n, start:stop]) + decode_square(got_middle[n, start:stop])
+                sum_code[n, start:stop] = encode(jnp.sqrt(2.0 * total))
+
+            @when_not(middle | outermost)
+            def receive():
+                to_total(n, s).wait_recv()
+
+            @when_not(outermost)
+            def pass_out():
+                to_total(n, s).start()
 
     coarse_halo = [halo(coarse_pack_ref.at[h], coarse_halo_ref.at[h], h) for h in range(2)]
     waves_halo = halo(pack_ref, halo_ref, 2)
@@ -297,7 +318,7 @@
             total = total + dot(segment(4 * h + g), spread[g])
         coarse_pack_ref[h] = total.astype(jnp.bfloat16)
         if h == 0:
-            pl.semaphore_wait(barrier, count + 1)
+            pl.semaphore_wait(barrier, 1 + jnp.where(outermost, 0, 1) + jnp.where(last_range, 0, 1))
         send_halo(coarse_halo[h])
     load_waves.wait()
     packed_keep = sum(dot(keep, s) for s in spread)[:1]
@@ -313,8 +334,9 @@
     fill_coefficients(coef_ref.at[tiles], octant, table)
     own = pick_own(column, boxes)
     fine_ref[ROWS - 1 : 4 * QUARTER, :] = jnp.zeros((4 * QUARTER - ROWS + 1, 128), jnp.float32)
-    pad = PIECE_ROWS - PIECE + 3
-    value_ref[:, PIECE_ROWS - pad : PIECE_ROWS, :] = jnp.zeros((pieces, pad, 128), jnp.float32)
+    for start in (4 * WIDTH - 4, PIECE_ROWS - 16):
+        stop = min(start + 16, PIECE_ROWS)
+        value_ref[:, start:stop, :] = jnp.zeros((pieces, stop - start, 128), jnp.float32)
 
     def leaf_coefficients(t, carry):
         fill_coefficients(coef_ref.at[t], local_keys(key2_ref[t], boxes)[1], valued)
@@ -389,13 +411,15 @@
         live = jnp.where(slot < counts_ref[0], 1.0, 0.0).astype(jnp.float32)
 
         def store_value(row, rows_in, value):
+            row = spread_row(row)
             value_ref[n, row : row + rows_in, :] = (value * live)[:rows_in]
 
         contract(part_b_ref, 0, 1, coef_ref.at[t], 2, store_value, **kinds)
 
         @pl.when(outermost)
         def start_chain():
-            send_partial(n, value_ref[n])
+            for s, (start, stop) in enumerate(SPLITS):
+                send_partial(n, s, value_ref[n, start:stop])
 
         if n >= LAG:
             combine(n - LAG)
@@ -413,15 +437,16 @@
             copy.wait_send()
 
     for n in range(pieces):
-        to_outer_slot(n).wait_send()
-
-        @when_not(outermost)
-        def totals_sent():
-            to_total(n).wait_send()
-
-        @pl.when(outermost & jnp.logical_not(middle))
-        def totals_received():
-            to_total(n).wait_recv()
+        for s in range(len(SPLITS)):
+            to_outer_slot(n, s).wait_send()
+
+            @when_not(outermost)
+            def totals_sent():
+                to_total(n, s).wait_send()
+
+            @pl.when(outermost & jnp.logical_not(middle))
+            def totals_received():
+                to_total(n, s).wait_recv()
 
 
 def decode_kernel(code_ref, out_hbm, piece_ref, value_ref, sem):
@@ -434,14 +459,15 @@
         )
 
     for n in range(pieces):
-        piece_ref[n, 0:SCALE_ROW, :] = decode_square(code_ref[n])
+        for start, stop in SPLITS:
+            piece_ref[n, start:stop, :] = decode_square(code_ref[n, start:stop])
     for n in range(pieces):
         t, part = n // PARTS, n % PARTS
         for f in range(3):
-            for k in range(11):
-                rows = min(8, 81 - 8 * k)
-                value = piece_ref[n, pl.ds(24 * k + f, rows, stride=3), :]
-                value_ref[t, pl.ds(72 * k + 3 * part + f, rows, stride=9), :] = value
+            for k in (*range(0, 36, 8), *range(36, 81, 8)):
+                rows = min(8, (36 if k < 36 else 81) - k)
+                value = piece_ref[n, pl.ds(spread_row(3 * k + f), rows, stride=3), :]
+                value_ref[t, pl.ds(9 * k + 3 * part + f, rows, stride=9), :] = value
         if part == PARTS - 1:
             out_copy(t).start()
     for t in range(tiles):
@@ -488,7 +514,7 @@
             pltpu.SemaphoreType.DMA((4,)),
             pltpu.SemaphoreType.DMA((4,)),
         ]
-        + [pltpu.SemaphoreType.DMA((pieces,))] * 5,
+        + [pltpu.SemaphoreType.DMA((pieces, len(SPLITS)))] * 5,
         compiler_params=pltpu.CompilerParams(
             collective_id=0, has_side_effects=True, vmem_limit_bytes=60 * 1024 * 1024
         ),

time: 39 us -> 37.9 us (0.972)
  Pallas kernels: 38.1 us -> 37.1 us
    pallas_call x1, Pallas kernels: 36.1 us -> 35.1 us  [shards(): pl.pallas_call(lambda *refs: density_kernel(*refs, count=count, ranges=ra...]
where the time goes in v2:
time: 37.9 us; the launch traced here: 37.7 us
  Pallas kernels  37.1 us (98%)
  between operations  0.66 us (2%)
    pallas_call x1, Pallas kernels, shards(): pl.pallas_call(lambda *refs: density_kernel(*refs, count=count, ranges=ra...  35.1 us
    pallas_call x1, Pallas kernels, shards(): pl.pallas_call(decode_kernel, out_shape=jax.ShapeDtypeStruct((ROWS, slots...  1.97 us

profile of v2, /device:TPU:4, one launch (start us, length us, event | category | flops | bytes accessed | tf_op | source)
XLA Modules:
  0.0 37.7 jit_solution(11245296590387588872)
XLA Ops:
  0.7 35.1 %shard_map.64.code_ref = s16[6,256,128]{2,1,0:T(8,128)(2,1)} custom-call(s32[1]{0:T(128)S(6)} %copy.7.refs_0_, bf16[729,8,128]{2,1,0:T(8,128)(2,1)} %bitcast.5, bf16[1,7,729,128]{3,2,1,0:T(8,128)(2,1)} %refs_2_.1, s32[1,128]{1,0:T(1,128)} %refs_3_.1, s32[1,128]{1,0:T(1,128)} %bitcast.7, s32[2,1,128]{2,1,0:T(1,128)} %bitcast.6), custom_call_target="tpu_custom_call" | custom-call | tf_op jit(solution)/shard_map/pallas_call | solution.py:487
  35.8 2.0 %shard_map.65 = f32[729,256]{1,0:T(8,128)} custom-call(s16[6,256,128]{2,1,0:T(8,128)(2,1)} %shard_map.64.code_ref), custom_call_target="tpu_custom_call" | custom-call | tf_op jit(solution)/shard_map/pallas_call | solution.py:529

commit v3 on v2

--- a/solution.py
+++ b/solution.py
@@ -82,8 +82,8 @@
 WIDTH = 27
 PIECE = 243
 PIECE_ROWS = 256
-SPLITS = ((0, 112), (112, 256))
-SHIFT = 4
+CUTS = (0, 5, 9)
+SPLITS = ((0, 144), (144, 256))
 PART_ROWS = 288
 LAG = 2
 
@@ -179,14 +179,16 @@
 
 
 def spread_row(row):
-    return row + (SHIFT if row >= 4 * WIDTH else 0)
+    for (start, stop), first, after in zip(SPLITS, CUTS, CUTS[1:]):
+        if row < after * WIDTH:
+            return row - first * WIDTH + start
 
 
 def density_kernel(
-    counts_ref, coarse_hbm, waves_hbm, flags_ref, key1_ref, key2_ref, sum_code,
-    coarse_ref, waves_ref, coarse_pack_ref, coarse_halo_ref, pack_ref, halo_ref, level_ref, fine_ref, spill_ref, spilled_ref,
+    counts_hbm, coarse_hbm, waves_hbm, flags_hbm, key1_hbm, key2_hbm, out_hbm,
+    counts_ref, flags_ref, key1_ref, key2_ref, sum_code, coarse_ref, waves_ref, coarse_pack_ref, coarse_halo_ref, pack_ref, halo_ref, level_ref, fine_ref, spill_ref, spilled_ref,
     x_ref, a_ref, b_ref, part_a_ref, part_b_ref, coef_ref, value_ref, code_ref, got_outer, got_middle,
-    load_sem, halo_send, halo_recv, code_send, outer_recv, middle_recv, sum_send, sum_recv, *, count, ranges, table, valued
+    load_sem, small_sem, out_sem, halo_send, halo_recv, code_send, outer_recv, middle_recv, sum_send, sum_recv, *, count, ranges, table, valued
 ):
     boxes = coarse_hbm.shape[-1]
     pieces = code_ref.shape[0]
@@ -200,10 +202,21 @@
     middle = (me == half - 1) | (me == half)
     first_range, last_range = position == 0, position == ranges - 1
     mesh_id = pl.DeviceIdType.MESH
-    load_coarse = pltpu.make_async_copy(coarse_hbm, coarse_ref.at[pl.ds(0, ROWS)], load_sem.at[0])
-    load_waves = pltpu.make_async_copy(waves_hbm, waves_ref, load_sem.at[1])
-    load_coarse.start()
-    load_waves.start()
+    load_coarse = []
+    for h in range(2):
+        rows_in = pl.ds(4 * SEGMENT * h, min(4 * SEGMENT, ROWS - 4 * SEGMENT * h))
+        load_coarse.append(pltpu.make_async_copy(coarse_hbm.at[rows_in], coarse_ref.at[rows_in], load_sem.at[h]))
+    load_waves = pltpu.make_async_copy(waves_hbm, waves_ref, load_sem.at[2])
+    for copy in (*load_coarse, load_waves):
+        copy.start()
+    small = [
+        pltpu.make_async_copy(source, target, small_sem.at[n])
+        for n, (source, target) in enumerate(
+            ((counts_hbm, counts_ref), (flags_hbm, flags_ref), (key1_hbm, key1_ref), (key2_hbm, key2_ref))
+        )
+    ]
+    for copy in small:
+        copy.start()
     barrier = pltpu.get_barrier_semaphore()
     pl.semaphore_signal(barrier, inc=1, device_id={"orb": inward}, device_id_type=mesh_id)
 
@@ -244,6 +257,9 @@
         part = part_of(sum_code, n, s)
         return remote(part, part, sum_send.at[n, s], sum_recv.at[n, s], {"orb": outward})
 
+    def put_out(n, s):
+        return pltpu.make_async_copy(part_of(sum_code, n, s), part_of(out_hbm, n, s), out_sem.at[n, s])
+
     def when_not(condition):
         return pl.when(jnp.logical_not(condition))
 
@@ -303,7 +319,6 @@
         for ref in (coarse_halo_ref, halo_ref, spilled_ref):
             ref[...] = jnp.zeros(ref.shape, ref.dtype)
 
-    keep = jnp.broadcast_to((1 - flags_ref[...]).astype(jnp.float32), (16, boxes)).astype(jnp.bfloat16)
     spread = [spread_matrix(boxes, g) for g in range(4)]
     tail = 8 * SEGMENT - ROWS
     coarse_ref[ROWS : ROWS + tail] = jnp.zeros((tail, 8, boxes), jnp.bfloat16)
@@ -311,8 +326,8 @@
     def segment(index):
         return coarse_ref[SEGMENT * index : SEGMENT * (index + 1)].reshape(8 * SEGMENT, boxes)
 
-    load_coarse.wait()
     for h in range(2):
+        load_coarse[h].wait()
         total = dot(segment(4 * h), spread[0])
         for g in range(1, 4):
             total = total + dot(segment(4 * h + g), spread[g])
@@ -321,6 +336,9 @@
             pl.semaphore_wait(barrier, 1 + jnp.where(outermost, 0, 1) + jnp.where(last_range, 0, 1))
         send_halo(coarse_halo[h])
     load_waves.wait()
+    for copy in small:
+        copy.wait()
+    keep = jnp.broadcast_to((1 - flags_ref[...]).astype(jnp.float32), (16, boxes)).astype(jnp.bfloat16)
     packed_keep = sum(dot(keep, s) for s in spread)[:1]
     for h in range(2):
         total = None
@@ -334,8 +352,8 @@
     fill_coefficients(coef_ref.at[tiles], octant, table)
     own = pick_own(column, boxes)
     fine_ref[ROWS - 1 : 4 * QUARTER, :] = jnp.zeros((4 * QUARTER - ROWS + 1, 128), jnp.float32)
-    for start in (4 * WIDTH - 4, PIECE_ROWS - 16):
-        stop = min(start + 16, PIECE_ROWS)
+    for (start, stop), first, after in zip(SPLITS, CUTS, CUTS[1:]):
+        start = (start + (after - first) * WIDTH) // 8 * 8
         value_ref[:, start:stop, :] = jnp.zeros((pieces, stop - start, 128), jnp.float32)
 
     def leaf_coefficients(t, carry):
@@ -431,27 +449,36 @@
         if 0 <= n - 2 * LAG:
             finish(n - 2 * LAG)
 
+    every = [(n, s) for n in range(pieces) for s in range(len(SPLITS))]
+    for n, s in every:
+
+        @pl.when(outermost & jnp.logical_not(middle))
+        def totals_received():
+            to_total(n, s).wait_recv()
+
+        put_out(n, s).start()
+
     @when_not(last_range)
     def halos_sent():
         for copy in (*coarse_halo, waves_halo, fine_halo):
             copy.wait_send()
 
-    for n in range(pieces):
-        for s in range(len(SPLITS)):
-            to_outer_slot(n, s).wait_send()
-
-            @when_not(outermost)
-            def totals_sent():
-                to_total(n, s).wait_send()
-
-            @pl.when(outermost & jnp.logical_not(middle))
-            def totals_received():
-                to_total(n, s).wait_recv()
-
-
-def decode_kernel(code_ref, out_hbm, piece_ref, value_ref, sem):
+    for n, s in every:
+        to_outer_slot(n, s).wait_send()
+
+        @when_not(outermost)
+        def totals_sent():
+            to_total(n, s).wait_send()
+
+        put_out(n, s).wait()
+
+
+def decode_kernel(code_hbm, out_hbm, code_ref, piece_ref, value_ref, in_sem, sem):
     pieces = code_ref.shape[0]
     tiles = pieces // PARTS
+    loads = [pltpu.make_async_copy(code_hbm.at[n], code_ref.at[n], in_sem.at[n]) for n in range(pieces)]
+    for copy in loads:
+        copy.start()
 
     def out_copy(t):
         return pltpu.make_async_copy(
@@ -459,15 +486,16 @@
         )
 
     for n in range(pieces):
+        t, part = n // PARTS, n % PARTS
+        loads[n].wait()
         for start, stop in SPLITS:
             piece_ref[n, start:stop, :] = decode_square(code_ref[n, start:stop])
-    for n in range(pieces):
-        t, part = n // PARTS, n % PARTS
         for f in range(3):
-            for k in (*range(0, 36, 8), *range(36, 81, 8)):
-                rows = min(8, (36 if k < 36 else 81) - k)
-                value = piece_ref[n, pl.ds(spread_row(3 * k + f), rows, stride=3), :]
-                value_ref[t, pl.ds(9 * k + 3 * part + f, rows, stride=9), :] = value
+            for first, after in zip(CUTS, CUTS[1:]):
+                for k in range(9 * first, 9 * after, 8):
+                    rows = min(8, 9 * after - k)
+                    value = piece_ref[n, pl.ds(spread_row(3 * k + f), rows, stride=3), :]
+                    value_ref[t, pl.ds(9 * k + 3 * part + f, rows, stride=9), :] = value
         if part == PARTS - 1:
             out_copy(t).start()
     for t in range(tiles):
@@ -482,14 +510,18 @@
     count, ranges = lax.axis_size("orb"), lax.axis_size("box")
     tiles = slots // 128
     pieces = PARTS * tiles
-    vmem = pl.BlockSpec(memory_space=pltpu.VMEM)
     anywhere = pl.BlockSpec(memory_space=pltpu.HBM)
     codes = pl.pallas_call(
         lambda *refs: density_kernel(*refs, count=count, ranges=ranges, table=matrix, valued=valued),
         out_shape=jax.ShapeDtypeStruct((pieces, PIECE_ROWS, 128), jnp.int16),
-        in_specs=[pl.BlockSpec(memory_space=pltpu.SMEM), anywhere, anywhere, vmem, vmem, vmem],
-        out_specs=vmem,
+        in_specs=[anywhere] * 6,
+        out_specs=anywhere,
         scratch_shapes=[
+            pltpu.SMEM((1,), jnp.int32),
+            pltpu.VMEM((1, boxes), jnp.int32),
+            pltpu.VMEM((1, boxes), jnp.int32),
+            pltpu.VMEM((tiles, 1, 128), jnp.int32),
+            pltpu.VMEM((pieces, PIECE_ROWS, 128), jnp.int16),
             pltpu.VMEM((8 * SEGMENT, 8, boxes), jnp.bfloat16),
             pltpu.VMEM(wavelets.shape, jnp.bfloat16),
             pltpu.VMEM((2, 8 * SEGMENT, 128), jnp.bfloat16),
@@ -510,7 +542,9 @@
             pltpu.VMEM((pieces, PIECE_ROWS, 128), jnp.int16),
             pltpu.VMEM((pieces, PIECE_ROWS, 128), jnp.int16),
             pltpu.VMEM((pieces, PIECE_ROWS, 128), jnp.int16),
-            pltpu.SemaphoreType.DMA((2,)),
+            pltpu.SemaphoreType.DMA((3,)),
+            pltpu.SemaphoreType.DMA((4,)),
+            pltpu.SemaphoreType.DMA((pieces, len(SPLITS))),
             pltpu.SemaphoreType.DMA((4,)),
             pltpu.SemaphoreType.DMA((4,)),
         ]
@@ -529,11 +563,13 @@
     return pl.pallas_call(
         decode_kernel,
         out_shape=jax.ShapeDtypeStruct((ROWS, slots), jnp.float32),
-        in_specs=[vmem],
+        in_specs=[anywhere],
         out_specs=anywhere,
         scratch_shapes=[
+            pltpu.VMEM((pieces, PIECE_ROWS, 128), jnp.int16),
             pltpu.VMEM((pieces, PIECE_ROWS, 128), jnp.float32),
             pltpu.VMEM((tiles, PADDED, 128), jnp.float32),
+            pltpu.SemaphoreType.DMA((pieces,)),
             pltpu.SemaphoreType.DMA((tiles,)),
         ],
     )(codes)

time: 37.9 us -> 37.2 us (0.982)
  Pallas kernels: 37.1 us -> 36.4 us
    pallas_call x1, Pallas kernels: 35.1 us -> 34.5 us  [shards(): pl.pallas_call(lambda *refs: density_kernel(*refs, count=count, ranges=ra...]
where the time goes in v3:
time: 37.2 us; the launch traced here: 37 us
  Pallas kernels  36.4 us (98%)
  between operations  0.66 us (2%)
    pallas_call x1, Pallas kernels, shards(): pl.pallas_call(lambda *refs: density_kernel(*refs, count=count, ranges=ra...  34.5 us
    pallas_call x1, Pallas kernels, shards(): pl.pallas_call(decode_kernel, out_shape=jax.ShapeDtypeStruct((ROWS, slots...  1.9 us

profile of v3, /device:TPU:4, one launch (start us, length us, event | category | flops | bytes accessed | tf_op | source)
XLA Modules:
  0.0 37.0 jit_solution(4906852510577431075)
XLA Ops:
  0.7 34.5 %shard_map.64.code_hbm = s16[6,256,128]{2,1,0:T(8,128)(2,1)} custom-call(s32[1]{0:T(128)S(6)} %copy.7.refs_0_, bf16[729,8,128]{2,1,0:T(8,128)(2,1)} %bitcast.5, bf16[1,7,729,128]{3,2,1,0:T(8,128)(2,1)} %refs_2_.1, s32[1,128]{1,0:T(1,128)} %refs_3_.1, s32[1,128]{1,0:T(1,128)} %bitcast.7, s32[2,1,128]{2,1,0:T(1,128)} %bitcast.6), custom_call_target="tpu_custom_call" | custom-call | tf_op jit(solution)/shard_map/pallas_call | solution.py:514
  35.1 1.9 %shard_map.65 = f32[729,256]{1,0:T(8,128)} custom-call(s16[6,256,128]{2,1,0:T(8,128)(2,1)} %shard_map.64.code_hbm), custom_call_target="tpu_custom_call" | custom-call | tf_op jit(solution)/shard_map/pallas_call | solution.py:563
